TPU v7x, 32 devices: a whole 2x2x4 slice. The times are simulated.
32 devices in a mesh: fsdp: 8 (over z, y), tp: 4 (over x, core).
Axes of the slice: x: 2, y: 2, z: 4, core: 2. Of those that a mesh axis runs over, the one named last changes fastest.
Arguments:
- inputs: bfloat16 [16, 736, 1152], P('fsdp', 'tp'), may hold values from -6 to 6
- cotangent: bfloat16 [16, 736, 1152], P('fsdp', 'tp'), may hold values from -6 to 6
- lengths: int32 [16], P('fsdp'), may hold values from 1 to 729, as said below
- ln1_gain: bfloat16 [1152], P('fsdp'), may hold values from 0.099609375 to 1.8984375
- ln1_bias: bfloat16 [1152], P('fsdp'), may hold values from -0.3125 to 0.3125
- q_weight: bfloat16 [1152, 1152], P('fsdp', 'tp'), may hold values from -0.1875 to 0.1875
- q_bias: bfloat16 [1152], P('tp'), may hold values from -3 to 3
- k_weight: bfloat16 [1152, 1152], P('fsdp', 'tp'), may hold values from -0.1875 to 0.1875
- v_weight: bfloat16 [1152, 1152], P('fsdp', 'tp'), may hold values from -0.1875 to 0.1875
- v_bias: bfloat16 [1152], P('tp'), may hold values from -0.1875 to 0.1875
- out_weight: bfloat16 [1152, 1152], P('tp', 'fsdp'), may hold values from -2.5 to 2.5
- out_bias: bfloat16 [1152], P('fsdp'), may hold values from -1.75 to 1.75
- ln2_gain: bfloat16 [1152], P('fsdp'), may hold values from 0.099609375 to 1.8984375
- ln2_bias: bfloat16 [1152], P('fsdp'), may hold values from -1.75 to 1.75
- up_weight: bfloat16 [1152, 4304], P('fsdp', 'tp'), may hold values from -0.1875 to 0.1875
- up_bias: bfloat16 [4304], P('tp'), may hold values from -1.75 to 1.75
- down_weight: bfloat16 [4304, 1152], P('tp', 'fsdp'), may hold values from -0.09375 to 0.09375
- down_bias: bfloat16 [1152], P('fsdp'), may hold values from -1.75 to 1.75
Outputs:
- layer_out: bfloat16 [16, 736, 1152], P('fsdp', 'tp')
- input_grad: float32 [16, 736, 1152], P('fsdp', 'tp')
- ln1_gain_grad: float32 [1152], P('fsdp')
- ln1_bias_grad: float32 [1152], P('fsdp')
- q_weight_grad: float32 [1152, 1152], P('fsdp', 'tp')
- q_bias_grad: float32 [1152], P('tp')
- k_weight_grad: float32 [1152, 1152], P('fsdp', 'tp')
- v_weight_grad: float32 [1152, 1152], P('fsdp', 'tp')
- v_bias_grad: float32 [1152], P('tp')
- out_weight_grad: float32 [1152, 1152], P('tp', 'fsdp')
- out_bias_grad: float32 [1152], P('fsdp')
- ln2_gain_grad: float32 [1152], P('fsdp')
- ln2_bias_grad: float32 [1152], P('fsdp')
- up_weight_grad: float32 [1152, 4304], P('fsdp', 'tp')
- up_bias_grad: float32 [4304], P('tp')
- down_weight_grad: float32 [4304, 1152], P('tp', 'fsdp')
- down_bias_grad: float32 [1152], P('fsdp')
Inputs may be any that keep to these rules, and one draw needn't show every extreme that they name: `lengths`: each slot either holds one image of 729 tokens or is empty with length 1; exactly 11 slots hold images, which ones drawn from the seed.
All inputs are finite; a program needn't handle non-finite values.
Results may differ from a plain program's by a relative error of at most 0.013.
Values may be sent and summed in bfloat16 or wider, within the bound.
No kernel may reach another device: no remote copies, remote signals or barrier semaphores. Data moves between devices by JAX's collectives and lax.ppermute only.
A program may use at most 192 MiB of HBM per device.

v0:
```python
import jax
import jax.numpy as jnp
from jax import lax
from jax.sharding import PartitionSpec as P

HD = 72
epsilon = 1e-06
negative_big = -1e30


def layer_norm(row_block, gain_vec, shift_vec):
    average = jnp.mean(row_block, -1, keepdims=True)
    center = row_block - average
    variance = jnp.mean(center * center, -1, keepdims=True)
    return center * lax.rsqrt(variance + epsilon) * gain_vec + shift_vec


def gelu_tanh(values_in):
    return jax.nn.gelu(values_in, approximate=True)


def plain_dot(left, right):
    return jnp.dot(left, right, preferred_element_type=jnp.float32)


def contract_rows(left, right):
    return lax.dot_general(
        left, right, (((0,), (0,)), ((), ())), preferred_element_type=jnp.float32
    )


def contract_cols(left, right):
    return lax.dot_general(
        left, right, (((1,), (1,)), ((), ())), preferred_element_type=jnp.float32
    )


def local(
    inputs,
    cotangent,
    lengths,
    ln1_gain,
    ln1_bias,
    q_weight,
    q_bias,
    k_weight,
    v_weight,
    v_bias,
    out_weight,
    out_bias,
    ln2_gain,
    ln2_bias,
    up_weight,
    up_bias,
    down_weight,
    down_bias,
):
    tp_count = lax.axis_size("tp")
    tp_index = lax.axis_index("tp")
    fsdp_index = lax.axis_index("fsdp")
    micro_count = inputs.shape[0]
    local_rows = inputs.shape[1]
    model_width = inputs.shape[2]
    seq_len = local_rows * tp_count
    head_width = q_weight.shape[1]
    heads_here = head_width // HD
    unit_width = up_weight.shape[1]
    scale_value = HD ** (-0.5)
    q_shift = q_bias.astype(jnp.float32)
    v_shift = v_bias.astype(jnp.float32)
    up_shift = up_bias.astype(jnp.float32)

    def fetch_weights():
        attn_full = (
            lax.all_gather(ln1_gain, "fsdp", axis=0, tiled=True),
            lax.all_gather(ln1_bias, "fsdp", axis=0, tiled=True),
            lax.all_gather(q_weight, "fsdp", axis=0, tiled=True),
            lax.all_gather(k_weight, "fsdp", axis=0, tiled=True),
            lax.all_gather(v_weight, "fsdp", axis=0, tiled=True),
            lax.all_gather(out_weight, "fsdp", axis=1, tiled=True),
            lax.all_gather(out_bias, "fsdp", axis=0, tiled=True),
        )
        mlp_full = (
            lax.all_gather(ln2_gain, "fsdp", axis=0, tiled=True),
            lax.all_gather(ln2_bias, "fsdp", axis=0, tiled=True),
            lax.all_gather(up_weight, "fsdp", axis=0, tiled=True),
            lax.all_gather(down_weight, "fsdp", axis=1, tiled=True),
            lax.all_gather(down_bias, "fsdp", axis=0, tiled=True),
        )
        return (attn_full, mlp_full)

    def masked_scores(queries, keys_all, key_valid):
        query_heads = queries.reshape(seq_len, heads_here, HD)
        key_heads = keys_all.reshape(seq_len, heads_here, HD)
        scores = (
            jnp.einsum("qhd,khd->hqk", query_heads, key_heads, preferred_element_type=jnp.float32)
            * scale_value
        )
        return jnp.where(key_valid[None, None, :], scores, negative_big)

    def forward(slot_rows, length, attn_full, mlp_full):
        gain_one, shift_one, wq_full, wk_full, wv_full, wo_full, bo_full = attn_full
        gain_two, shift_two, w_up, w_down, bd_full = mlp_full
        key_valid = jnp.arange(seq_len, dtype=jnp.int32) < length
        norm_one = layer_norm(
            slot_rows, gain_one.astype(jnp.float32), shift_one.astype(jnp.float32)
        ).astype(jnp.bfloat16)
        norm_full = lax.all_gather(norm_one, "tp", axis=0, tiled=True)
        queries = (plain_dot(norm_full, wq_full) + q_shift).astype(jnp.bfloat16)
        keys_all = plain_dot(norm_full, wk_full).astype(jnp.bfloat16)
        values_all = (plain_dot(norm_full, wv_full) + v_shift).astype(jnp.bfloat16)
        scores = masked_scores(queries, keys_all, key_valid)
        row_max = jnp.max(scores, -1, keepdims=True)
        row_total = jnp.sum(jnp.exp(scores - row_max), -1, keepdims=True)
        log_total = row_max + jnp.log(row_total)
        soft_low = jnp.exp(scores - log_total).astype(jnp.bfloat16)
        value_heads = values_all.reshape(seq_len, heads_here, HD)
        mixed_heads = jnp.einsum(
            "hqk,khd->qhd", soft_low, value_heads, preferred_element_type=jnp.float32
        )
        mixed_heads = mixed_heads.astype(jnp.bfloat16).reshape(seq_len, head_width)
        attended = lax.psum_scatter(
            plain_dot(mixed_heads, wo_full), "tp", scatter_dimension=0, tiled=True
        )
        middle = slot_rows + attended + bo_full.astype(jnp.float32)
        norm_two = layer_norm(
            middle, gain_two.astype(jnp.float32), shift_two.astype(jnp.float32)
        ).astype(jnp.bfloat16)
        norm_two_full = lax.all_gather(norm_two, "tp", axis=0, tiled=True)
        hidden = plain_dot(norm_two_full, w_up) + up_shift
        active = gelu_tanh(hidden).astype(jnp.bfloat16)
        mlp_rows = lax.psum_scatter(
            plain_dot(active, w_down), "tp", scatter_dimension=0, tiled=True
        )
        out_rows = middle + mlp_rows + bd_full.astype(jnp.float32)
        kept_state = (
            norm_full,
            queries,
            keys_all,
            values_all,
            log_total,
            mixed_heads,
            middle,
            norm_two_full,
            hidden,
            active,
        )
        return (out_rows, kept_state)

    outputs = []
    for slot_index in range(micro_count):
        attn_full, mlp_full = fetch_weights()
        out_rows, kept_state = forward(
            inputs[slot_index].astype(jnp.float32), lengths[slot_index], attn_full, mlp_full
        )
        outputs.append(out_rows.astype(jnp.bfloat16))
    grad_list = []
    totals = None
    for slot_index in range(micro_count):
        attn_full, mlp_full = fetch_weights()
        slot_rows = inputs[slot_index].astype(jnp.float32)
        kept_state = forward(slot_rows, lengths[slot_index], attn_full, mlp_full)[1]
        backward_length = lengths[slot_index]
        (
            backward_gain_one,
            backward_shift_one,
            backward_wq_full,
            backward_wk_full,
            backward_wv_full,
            backward_wo_full,
            backward_bo_full,
        ) = attn_full
        backward_gain_two, backward_shift_two, backward_w_up, backward_w_down, backward_bd_full = (
            mlp_full
        )
        (
            backward_norm_full,
            backward_queries,
            backward_keys_all,
            backward_values_all,
            backward_log_total,
            backward_mixed_heads,
            backward_middle,
            backward_norm_two_full,
            backward_hidden,
            backward_active,
        ) = kept_state
        backward_key_valid = jnp.arange(seq_len, dtype=jnp.int32) < backward_length
        row_valid = (
            jnp.arange(local_rows, dtype=jnp.int32) + tp_index * local_rows < backward_length
        ).astype(jnp.float32)
        grad_out = cotangent[slot_index].astype(jnp.float32) * row_valid[:, None]
        backward_down_sum = jnp.sum(grad_out, 0)
        grad_out_full = lax.all_gather(grad_out.astype(jnp.bfloat16), "tp", axis=0, tiled=True)
        backward_grad_w_down = contract_rows(backward_active, grad_out_full)
        grad_active = contract_cols(grad_out_full, backward_w_down)
        gelu_pull = jax.vjp(gelu_tanh, backward_hidden)[1]
        grad_hidden = gelu_pull(grad_active)[0].astype(jnp.bfloat16)
        backward_up_sum = jnp.sum(grad_hidden.astype(jnp.float32), 0)
        backward_grad_w_up = contract_rows(backward_norm_two_full, grad_hidden)
        grad_norm_two = lax.psum_scatter(
            contract_cols(grad_hidden, backward_w_up), "tp", scatter_dimension=0, tiled=True
        )
        norm_two_pull = jax.vjp(
            layer_norm,
            backward_middle,
            backward_gain_two.astype(jnp.float32),
            backward_shift_two.astype(jnp.float32),
        )[1]
        middle_part, backward_gain_two_grad, backward_shift_two_grad = norm_two_pull(grad_norm_two)
        grad_middle = grad_out + middle_part
        backward_out_sum = jnp.sum(grad_middle, 0)
        grad_middle_full = lax.all_gather(
            grad_middle.astype(jnp.bfloat16), "tp", axis=0, tiled=True
        )
        backward_grad_w_out = contract_rows(backward_mixed_heads, grad_middle_full)
        grad_mixed = (
            contract_cols(grad_middle_full, backward_wo_full)
            .astype(jnp.bfloat16)
            .reshape(seq_len, heads_here, HD)
        )
        soft_weights = jnp.exp(
            masked_scores(backward_queries, backward_keys_all, backward_key_valid)
            - backward_log_total
        )
        backward_soft_low = soft_weights.astype(jnp.bfloat16)
        backward_query_heads = backward_queries.reshape(seq_len, heads_here, HD)
        backward_key_heads = backward_keys_all.reshape(seq_len, heads_here, HD)
        backward_value_heads = backward_values_all.reshape(seq_len, heads_here, HD)
        grad_soft = jnp.einsum(
            "qhd,khd->hqk", grad_mixed, backward_value_heads, preferred_element_type=jnp.float32
        )
        row_inner = jnp.sum(soft_weights * grad_soft, -1, keepdims=True)
        grad_scores = (soft_weights * (grad_soft - row_inner)).astype(jnp.bfloat16)
        grad_queries = (
            (
                jnp.einsum(
                    "hqk,khd->qhd",
                    grad_scores,
                    backward_key_heads,
                    preferred_element_type=jnp.float32,
                )
                * scale_value
            )
            .astype(jnp.bfloat16)
            .reshape(seq_len, head_width)
        )
        grad_keys = (
            (
                jnp.einsum(
                    "hqk,qhd->khd",
                    grad_scores,
                    backward_query_heads,
                    preferred_element_type=jnp.float32,
                )
                * scale_value
            )
            .astype(jnp.bfloat16)
            .reshape(seq_len, head_width)
        )
        grad_values = (
            jnp.einsum(
                "hqk,qhd->khd", backward_soft_low, grad_mixed, preferred_element_type=jnp.float32
            )
            .astype(jnp.bfloat16)
            .reshape(seq_len, head_width)
        )
        backward_query_sum = jnp.sum(grad_queries.astype(jnp.float32), 0)
        backward_value_sum = jnp.sum(grad_values.astype(jnp.float32), 0)
        backward_grad_wq = contract_rows(backward_norm_full, grad_queries)
        backward_grad_wk = contract_rows(backward_norm_full, grad_keys)
        backward_grad_wv = contract_rows(backward_norm_full, grad_values)
        part_q = contract_cols(grad_queries, backward_wq_full)
        part_k = contract_cols(grad_keys, backward_wk_full)
        part_v = contract_cols(grad_values, backward_wv_full)
        grad_norm_one = lax.psum_scatter(
            part_q + part_k + part_v, "tp", scatter_dimension=0, tiled=True
        )
        norm_one_pull = jax.vjp(
            layer_norm,
            slot_rows,
            backward_gain_one.astype(jnp.float32),
            backward_shift_one.astype(jnp.float32),
        )[1]
        rows_part, backward_gain_one_grad, backward_shift_one_grad = norm_one_pull(grad_norm_one)
        grad_rows = grad_middle + rows_part
        slot_grads = (
            backward_gain_one_grad,
            backward_shift_one_grad,
            backward_grad_wq,
            backward_query_sum,
            backward_grad_wk,
            backward_grad_wv,
            backward_value_sum,
            backward_grad_w_out,
            backward_out_sum,
            backward_gain_two_grad,
            backward_shift_two_grad,
            backward_grad_w_up,
            backward_up_sum,
            backward_grad_w_down,
            backward_down_sum,
        )
        grad_rows, slot_grads = (grad_rows, slot_grads)
        grad_list.append(grad_rows)
        if totals is None:
            totals = slot_grads
        else:
            totals = jax.tree.map(jnp.add, totals, slot_grads)
    (
        gain_one_grad,
        shift_one_grad,
        grad_wq,
        query_sum,
        grad_wk,
        grad_wv,
        value_sum,
        grad_w_out,
        out_sum,
        gain_two_grad,
        shift_two_grad,
        grad_w_up,
        up_sum,
        grad_w_down,
        down_sum,
    ) = totals
    summed_weights = (
        lax.psum_scatter(grad_wq, "fsdp", scatter_dimension=0, tiled=True),
        lax.psum_scatter(grad_wk, "fsdp", scatter_dimension=0, tiled=True),
        lax.psum_scatter(grad_wv, "fsdp", scatter_dimension=0, tiled=True),
        lax.psum_scatter(grad_w_out, "fsdp", scatter_dimension=1, tiled=True),
        lax.psum_scatter(grad_w_up, "fsdp", scatter_dimension=0, tiled=True),
        lax.psum_scatter(grad_w_down, "fsdp", scatter_dimension=1, tiled=True),
    )
    width_stack = jnp.stack(
        [gain_one_grad, shift_one_grad, out_sum, gain_two_grad, shift_two_grad, down_sum], 0
    )
    head_stack = jnp.zeros((2, head_width * tp_count), jnp.float32)
    head_stack = lax.dynamic_update_slice_in_dim(
        head_stack, jnp.stack([query_sum, value_sum], 0), tp_index * head_width, 1
    )
    unit_line = jnp.zeros((unit_width * tp_count,), jnp.float32)
    unit_line = lax.dynamic_update_slice_in_dim(unit_line, up_sum, tp_index * unit_width, 0)
    summed_small = lax.psum((width_stack, head_stack, unit_line), ("fsdp", "tp"))
    shard_size = model_width // lax.axis_size("fsdp")
    width_pieces = lax.dynamic_slice_in_dim(summed_small[0], fsdp_index * shard_size, shard_size, 1)
    head_pieces = lax.dynamic_slice_in_dim(summed_small[1], tp_index * head_width, head_width, 1)
    unit_piece = lax.dynamic_slice_in_dim(summed_small[2], tp_index * unit_width, unit_width, 0)
    return (
        jnp.stack(outputs, 0),
        jnp.stack(grad_list, 0),
        width_pieces[0],
        width_pieces[1],
        summed_weights[0],
        head_pieces[0],
        summed_weights[1],
        summed_weights[2],
        head_pieces[1],
        summed_weights[3],
        width_pieces[2],
        width_pieces[3],
        width_pieces[4],
        summed_weights[4],
        unit_piece,
        summed_weights[5],
        width_pieces[5],
    )


def solution(mesh):
    in_specs = (
        P("fsdp", "tp", None),
        P("fsdp", "tp", None),
        P("fsdp"),
        P("fsdp"),
        P("fsdp"),
        P("fsdp", "tp"),
        P("tp"),
        P("fsdp", "tp"),
        P("fsdp", "tp"),
        P("tp"),
        P("tp", "fsdp"),
        P("fsdp"),
        P("fsdp"),
        P("fsdp"),
        P("fsdp", "tp"),
        P("tp"),
        P("tp", "fsdp"),
        P("fsdp"),
    )
    out_specs = (
        P("fsdp", "tp", None),
        P("fsdp", "tp", None),
        P("fsdp"),
        P("fsdp"),
        P("fsdp", "tp"),
        P("tp"),
        P("fsdp", "tp"),
        P("fsdp", "tp"),
        P("tp"),
        P("tp", "fsdp"),
        P("fsdp"),
        P("fsdp"),
        P("fsdp"),
        P("fsdp", "tp"),
        P("tp"),
        P("tp", "fsdp"),
        P("fsdp"),
    )
    return jax.shard_map(local, mesh=mesh, in_specs=in_specs, out_specs=out_specs, check_vma=False)
```

profile of v0, /device:TPU:0, one launch (start us, length us, event | category | flops | bytes accessed | tf_op | source)
XLA Modules:
  0.0 1294.0 jit_solution(5558494795576318744)
XLA Ops:
  14.4 38.8 %all-reduce.15 = (bf16[1152]{0:T(1024)(128)(2,1)S(1)}, bf16[1152]{0:T(1024)(128)(2,1)S(1)}, bf16[1152]{0:T(1024)(128)(2,1)S(1)}, bf16[1152]{0:T(1024)(128)(2,1)S...) all-reduce(bf16[1152]{0:T(1024)(128)(2,1)S(1)} %dynamic-update-slic, ...), channel_id=1, replica_groups=mesh['fsdp'=8,'tp'=4] {'fsdp'}, use_global_device_ids=true, to_apply=%add.1 | all-reduce | flops 6912 | bytes 27648
  60.0 32.5 %all_gather.44 = bf16[1152,288]{1,0:T(8,128)(2,1)S(1)} all-gather(bf16[144,288]{1,0:T(8,128)(2,1)S(1)} %copy-done.54), channel_id=1, replica_groups=mesh['fsdp'=8,'tp'=4] {'fsdp'}, dimensions={0}, use_global_device_ids=true | all-gather | bytes 746496 | tf_op jit(solution)/shard_map/all_gather | solution.py:77
  92.5 32.2 %all_gather.45 = bf16[1152,288]{1,0:T(8,128)(2,1)S(1)} all-gather(bf16[144,288]{1,0:T(8,128)(2,1)S(1)} %copy-done.55), channel_id=1, replica_groups=mesh['fsdp'=8,'tp'=4] {'fsdp'}, dimensions={0}, use_global_device_ids=true | all-gather | bytes 746496 | tf_op jit(solution)/shard_map/all_gather | solution.py:78
  126.1 34.5 %all_gather.43 = bf16[1152,288]{1,0:T(8,128)(2,1)} all-gather(bf16[144,288]{1,0:T(8,128)(2,1)S(1)} %copy-done.56), channel_id=1, replica_groups=mesh['fsdp'=8,'tp'=4] {'fsdp'}, dimensions={0}, use_global_device_ids=true | all-gather | bytes 746496 | tf_op jit(solution)/shard_map/all_gather | solution.py:79
  160.6 32.0 %all_gather.46 = bf16[288,1152]{0,1:T(8,128)(2,1)S(1)} all-gather(bf16[288,144]{0,1:T(8,128)(2,1)S(1)} %copy-done.57), channel_id=1, replica_groups=mesh['fsdp'=8,'tp'=4] {'fsdp'}, dimensions={1}, use_global_device_ids=true | all-gather | bytes 746496 | tf_op jit(solution)/shard_map/all_gather | solution.py:80
  231.9 15.0 %reduce-scatter.47.cloned.1.call-done = f32[184,1152]{1,0:T(8,128)} async-done(((f32[736,1152]{1,0:T(8,128)}), f32[184,1152]{1,0:T(8,128)}) %reduce-scatter.47.cloned.1.call-update) | async-done | bytes 847888
  247.0 42.0 %reduce-scatter.43.cloned.1.call-done = f32[184,1152]{1,0:T(8,128)} async-done(((f32[736,1152]{1,0:T(8,128)}), f32[184,1152]{1,0:T(8,128)}) %reduce-scatter.43.cloned.1.call-update) | async-done | bytes 847888
  294.4 17.0 %all-gather.23.cloned.1.call-done = bf16[736,1152]{1,0:T(8,128)(2,1)} async-done(((bf16[184,1152]{1,0:T(8,128)(2,1)}), bf16[736,1152]{1,0:T(8,128)(2,1)}) %all-gather.23.cloned.1.call-update) | async-done | bytes 1695760 | tf_op jit(solution)/shard_map/all_gather | solution.py:194
  311.4 57.1 %all-gather.17.cloned.1.call-done = bf16[1076,1152]{0,1:T(8,128)(2,1)} async-done(((bf16[1076,144]{0,1:T(8,128)(2,1)}), bf16[1076,1152]{0,1:T(8,128)(2,1)}) %all-gather.17.cloned.1.call-update) | async-done | bytes 2479120 | tf_op jit(solution)/shard_map/all_gather | solution.py:87
  368.5 6.4 fusion.87
  374.9 49.4 %all-gather.15.cloned.1.call-done = bf16[1152,1076]{1,0:T(8,128)(2,1)} async-done(((bf16[144,1076]{1,0:T(8,128)(2,1)}), bf16[1152,1076]{1,0:T(8,128)(2,1)}) %all-gather.15.cloned.1.call-update) | async-done | bytes 2479120 | tf_op jit(solution)/shard_map/all_gather | solution.py:86
  424.3 20.5 %all-gather.13.cloned.1.call-done = bf16[736,1152]{1,0:T(8,128)(2,1)} async-done(((bf16[184,1152]{1,0:T(8,128)(2,1)}), bf16[736,1152]{1,0:T(8,128)(2,1)}) %all-gather.13.cloned.1.call-update) | async-done | bytes 1695760 | tf_op jit(solution)/shard_map/all_gather | solution.py:129
  444.8 10.3 convert_reduce_fusion.1
  466.7 6.4 fusion.90
  473.1 15.4 %all-gather.21.cloned.1.call-done = bf16[736,1152]{1,0:T(8,128)(2,1)} async-done(((bf16[184,1152]{1,0:T(8,128)(2,1)}), bf16[736,1152]{1,0:T(8,128)(2,1)}) %all-gather.21.cloned.1.call-update) | async-done | bytes 1695760 | tf_op jit(solution)/shard_map/all_gather | solution.py:129
  488.5 10.2 convert_reduce_fusion
  504.6 7.8 fusion.73
  512.5 7.6 fusion.74
  520.2 10.4 reduce-scatter.51.cloned.1.call-done
  530.6 42.1 %reduce-scatter.55.cloned.1.call-done = f32[184,1152]{1,0:T(8,128)} async-done(((f32[736,1152]{1,0:T(8,128)}), f32[184,1152]{1,0:T(8,128)}) %reduce-scatter.55.cloned.1.call-update) | async-done | bytes 847888
  574.8 39.9 %reduce-scatter.45.cloned.1.call-done = f32[184,1152]{1,0:T(8,128)} async-done(((f32[736,1152]{1,0:T(8,128)}), f32[184,1152]{1,0:T(8,128)}) %reduce-scatter.45.cloned.1.call-update) | async-done | bytes 847888
  614.7 42.1 %reduce-scatter.49.cloned.1.call-done = f32[184,1152]{1,0:T(8,128)} async-done(((f32[736,1152]{1,0:T(8,128)}), f32[184,1152]{1,0:T(8,128)}) %reduce-scatter.49.cloned.1.call-update) | async-done | bytes 847888
  665.4 19.5 %all-gather.29.cloned.1.call-done = bf16[736,1152]{1,0:T(8,128)(2,1)} async-done(((bf16[184,1152]{1,0:T(8,128)(2,1)}), bf16[736,1152]{1,0:T(8,128)(2,1)}) %all-gather.29.cloned.1.call-update) | async-done | bytes 1695760 | tf_op jit(solution)/shard_map/all_gather | solution.py:213
  713.2 6.6 multiply_reduce_fusion.1
  782.2 9.3 reduce-scatter.53.cloned.1.call-done
  796.5 43.7 %all-reduce.14 = (f32[6,1152]{1,0:T(8,128)}, f32[2,1152]{1,0:T(2,128)S(1)}, f32[4304]{0:T(1024)S(1)}) all-reduce(f32[6,1152]{1,0:T(8,128)S(1)} %stack.38, f32[2,1152]{1,0:T(2,128)S(1)} %dynamic_update_slice.6, f32[4304]{0:T(1024)S(1)} %add_dynamic-update-slice_fusion), channel_id=1, replica_groups=mesh['fsdp'=8,'tp'=4] {'fsdp','tp'}, use_global_device_ids=true, to_apply=%region_42.43 | all-reduce | flops 13520 | bytes 108160 | tf_op jit(solution)/shard_map/psum | solution.py:344
  848.7 52.2 %reduce-scatter.39.cloned.1.call-done = f32[144,1076]{1,0:T(8,128)} async-done(((f32[1152,1076]{1,0:T(8,128)}), f32[144,1076]{1,0:T(8,128)}) %reduce-scatter.39.cloned.1.call-update) | async-done | bytes 619792 | tf_op jit(solution)/shard_map/reduce_scatter | solution.py:332
  901.0 108.4 %reduce-scatter.41.cloned.1.call-done = f32[1076,144]{0,1:T(8,128)} async-done(((f32[1076,1152]{0,1:T(8,128)}), f32[1076,144]{0,1:T(8,128)}) %reduce-scatter.41.cloned.1.call-update) | async-done | bytes 619792 | tf_op jit(solution)/shard_map/reduce_scatter | solution.py:333
  1009.4 69.9 %reduce-scatter.37.cloned.1.call-done = f32[288,144]{0,1:T(8,128)} async-done(((f32[288,1152]{0,1:T(8,128)}), f32[288,144]{0,1:T(8,128)}) %reduce-scatter.37.cloned.1.call-update) | async-done | bytes 165904 | tf_op jit(solution)/shard_map/reduce_scatter | solution.py:331
  1079.3 69.5 %reduce-scatter.35.cloned.1.call-done = f32[144,288]{1,0:T(8,128)} async-done(((f32[1152,288]{1,0:T(8,128)}), f32[144,288]{1,0:T(8,128)}) %reduce-scatter.35.cloned.1.call-update) | async-done | bytes 165904 | tf_op jit(solution)/shard_map/reduce_scatter | solution.py:330
  1148.7 69.0 %reduce-scatter.33.cloned.1.call-done = f32[144,288]{1,0:T(8,128)} async-done(((f32[1152,288]{1,0:T(8,128)}), f32[144,288]{1,0:T(8,128)}) %reduce-scatter.33.cloned.1.call-update) | async-done | bytes 165904 | tf_op jit(solution)/shard_map/reduce_scatter | solution.py:329
  1217.7 69.0 %reduce-scatter.31.cloned.1.call-done = f32[144,288]{1,0:T(8,128)} async-done(((f32[1152,288]{1,0:T(8,128)}), f32[144,288]{1,0:T(8,128)}) %reduce-scatter.31.cloned.1.call-update) | async-done | bytes 165904 | tf_op jit(solution)/shard_map/reduce_scatter | solution.py:328
  (417 shorter events, 190.1 us)
Async XLA Ops:
  7.2 85.3 %copy-start.91 = (bf16[288]{0:T(512)(128)(2,1)S(1)}, bf16[288]{0:T(512)(128)(2,1)}, u32[]{:S(2)}) copy-start(bf16[288]{0:T(512)(128)(2,1)} %param.24) | copy-start | bytes 1732
  7.2 117.5 %copy-start.90 = (s32[2]{0:T(128)S(1)}, s32[2]{0:T(128)}, u32[]{:S(2)}) copy-start(s32[2]{0:T(128)} %param.20) | copy-start | bytes 28
  7.2 118.8 %copy-start.56 = (bf16[144,288]{1,0:T(8,128)(2,1)S(1)}, bf16[144,288]{1,0:T(8,128)(2,1)}, u32[]{:S(2)}) copy-start(bf16[144,288]{1,0:T(8,128)(2,1)} %param.26) | copy-start | bytes 248836
  7.2 185.3 %all-gather.19.cloned.1.call-start = ((), (), s32[]{:S(2)}) async-start(), calls=%async_computation.18 | async-start | bytes 2119680 | tf_op jit(solution)/shard_map/all_gather | solution.py:108
  54.6 106.0 %copy-start.92 = (bf16[288]{0:T(512)(128)(2,1)S(1)}, bf16[288]{0:T(512)(128)(2,1)}, u32[]{:S(2)}) copy-start(bf16[288]{0:T(512)(128)(2,1)} %param.27) | copy-start | bytes 1732
  54.6 106.0 %copy-start.57 = (bf16[288,144]{0,1:T(8,128)(2,1)S(1)}, bf16[288,144]{0,1:T(8,128)(2,1)}, u32[]{:S(2)}) copy-start(bf16[288,144]{0,1:T(8,128)(2,1)} %param.28) | copy-start | bytes 248836
  59.2 151.7 %all-gather.11.cloned.1.call-start = ((), (), s32[]{:S(2)}) async-start(), calls=%async_computation.14 | async-start | bytes 2119680 | tf_op jit(solution)/shard_map/all_gather | solution.py:108
  60.0 187.0 %reduce-scatter.47.cloned.1.call-start = ((), (), s32[]{:S(2)}) async-start(), calls=%async_computation.32 | async-start | bytes 4239360
  124.7 86.1 %copy-start.11 = (bf16[1152,288]{1,0:T(8,128)(2,1)}, bf16[1152,288]{1,0:T(8,128)(2,1)S(1)}, u32[]{:S(2)}) copy-start(bf16[1152,288]{1,0:T(8,128)(2,1)S(1)} %all_gather.45) | copy-start | bytes 1990660
  209.9 79.2 %reduce-scatter.43.cloned.1.call-start = ((), (), s32[]{:S(2)}) async-start(), calls=%async_computation.30 | async-start | bytes 4239360
  227.8 83.6 %all-gather.23.cloned.1.call-start = ((), (), s32[]{:S(2)}) async-start(), calls=%async_computation.20 | async-start | bytes 2119680 | tf_op jit(solution)/shard_map/all_gather | solution.py:194
  230.5 138.0 %all-gather.17.cloned.1.call-start = ((), (), s32[]{:S(2)}) async-start(), calls=%async_computation.17 | async-start | bytes 2985984 | tf_op jit(solution)/shard_map/all_gather | solution.py:87
  231.1 193.2 %all-gather.15.cloned.1.call-start = ((), (), s32[]{:S(2)}) async-start(), calls=%async_computation.16 | async-start | bytes 2985984 | tf_op jit(solution)/shard_map/all_gather | solution.py:86
  231.8 213.0 %all-gather.13.cloned.1.call-start = ((), (), s32[]{:S(2)}) async-start(), calls=%async_computation.15 | async-start | bytes 2119680 | tf_op jit(solution)/shard_map/all_gather | solution.py:129
  292.6 174.2 %all-gather.27.cloned.1.call-start = ((), (), s32[]{:S(2)}) async-start(), calls=%async_computation.22 | async-start | bytes 2119680 | tf_op jit(solution)/shard_map/all_gather | solution.py:194
  293.3 195.2 %all-gather.21.cloned.1.call-start = ((), (), s32[]{:S(2)}) async-start(), calls=%async_computation.19 | async-start | bytes 2119680 | tf_op jit(solution)/shard_map/all_gather | solution.py:129
  293.9 236.7 %reduce-scatter.51.cloned.1.call-start = ((), (), s32[]{:S(2)}) async-start(), calls=%async_computation.34 | async-start | bytes 4239360
  460.8 111.9 %reduce-scatter.55.cloned.1.call-start = ((), (), s32[]{:S(2)}) async-start(), calls=%async_computation.36 | async-start | bytes 4239360
  504.3 110.3 %reduce-scatter.45.cloned.1.call-start = ((), (), s32[]{:S(2)}) async-start(), calls=%async_computation.31 | async-start | bytes 4239360
  512.4 144.3 %reduce-scatter.49.cloned.1.call-start = ((), (), s32[]{:S(2)}) async-start(), calls=%async_computation.33 | async-start | bytes 4239360
  520.1 164.7 %all-gather.29.cloned.1.call-start = ((), (), s32[]{:S(2)}) async-start(), calls=%async_computation.23 | async-start | bytes 2119680 | tf_op jit(solution)/shard_map/all_gather | solution.py:213
  574.7 86.5 %copy-start.72 = (f32[184]{0:T(256)S(1)}, f32[184]{0:T(256)}, u32[]{:S(2)}) copy-start(f32[184]{0:T(256)} %copy-done.71) | copy-start | bytes 2212
  574.7 86.5 %copy-start.75 = (f32[184]{0:T(256)S(1)}, f32[184]{0:T(256)}, u32[]{:S(2)}) copy-start(f32[184]{0:T(256)} %copy-done.74) | copy-start | bytes 2212
  664.4 45.6 %all-gather.25.cloned.1.call-start = ((), (), s32[]{:S(2)}) async-start(), calls=%async_computation.21 | async-start | bytes 2119680 | tf_op jit(solution)/shard_map/all_gather | solution.py:213
  665.0 117.2 %reduce-scatter.57.cloned.1.call-start = ((), (), s32[]{:S(2)}) async-start(), calls=%async_computation.37 | async-start | bytes 4239360
  709.8 81.7 %reduce-scatter.53.cloned.1.call-start = ((), (), s32[]{:S(2)}) async-start(), calls=%async_computation.35 | async-start | bytes 4239360
  734.7 166.2 %reduce-scatter.39.cloned.1.call-start = ((), (), s32[]{:S(2)}) async-start(), calls=%async_computation.28 | async-start | bytes 5971968 | tf_op jit(solution)/shard_map/reduce_scatter | solution.py:332
  745.5 263.9 %reduce-scatter.41.cloned.1.call-start = ((), (), s32[]{:S(2)}) async-start(), calls=%async_computation.29 | async-start | bytes 5971968 | tf_op jit(solution)/shard_map/reduce_scatter | solution.py:333
  756.8 322.4 %reduce-scatter.37.cloned.1.call-start = ((), (), s32[]{:S(2)}) async-start(), calls=%async_computation.27 | async-start | bytes 1990656 | tf_op jit(solution)/shard_map/reduce_scatter | solution.py:331
  763.1 385.7 %reduce-scatter.35.cloned.1.call-start = ((), (), s32[]{:S(2)}) async-start(), calls=%async_computation.26 | async-start | bytes 1990656 | tf_op jit(solution)/shard_map/reduce_scatter | solution.py:330
  768.3 449.4 %reduce-scatter.33.cloned.1.call-start = ((), (), s32[]{:S(2)}) async-start(), calls=%async_computation.25 | async-start | bytes 1990656 | tf_op jit(solution)/shard_map/reduce_scatter | solution.py:329
  773.5 513.2 %reduce-scatter.31.cloned.1.call-start = ((), (), s32[]{:S(2)}) async-start(), calls=%async_computation.24 | async-start | bytes 1990656 | tf_op jit(solution)/shard_map/reduce_scatter | solution.py:328
  (106 other events, 1012.5 us)
Sparse Core Ops, SparseCore 0:
  59.3 17.5 all-gather.18
  79.0 20.3 all-gather.10
  210.0 36.9 reduce-scatter.46
  249.5 39.4 reduce-scatter.42
  291.0 20.3 all-gather.22
  313.4 55.0 all-gather.16
  370.6 53.5 all-gather.14
  425.8 18.9 all-gather.12
  446.4 20.3 all-gather.26
  468.1 20.3 all-gather.20
  491.1 39.4 reduce-scatter.50
  533.1 39.4 reduce-scatter.54
  575.2 39.4 reduce-scatter.44
  617.2 39.4 reduce-scatter.48
  664.5 20.3 all-gather.28
  686.3 20.3 all-gather.24
  709.9 39.4 reduce-scatter.56
  752.0 39.4 reduce-scatter.52
  795.6 105.2 reduce-scatter.38
  905.4 103.9 reduce-scatter.40
  1013.4 65.7 reduce-scatter.36
  1083.7 64.9 reduce-scatter.34
  1152.8 64.8 reduce-scatter.32
  1222.0 64.6 reduce-scatter.30
where the time goes:
time: 1300 us; the launch traced here: 1290 us
  waiting for transfers between devices  827 us (64%)
  blocking collectives  214 us (16%)
  matrix products  156 us (12%)
  other arithmetic  50 us (4%)
  local copies, waits for them, and re-layouts  26.7 us (2%)
  between operations  17.3 us (1%)
    unnamed x32, waiting for transfers between devices  205 us
    reduce_scatter x1, waiting for transfers between devices, local(): lax.psum_scatter(grad_w_down, 'fsdp', scatter_dimension=1, tiled=True)  108 us
    reduce_scatter x1, waiting for transfers between devices, local(): lax.psum_scatter(grad_w_out, 'fsdp', scatter_dimension=1, tiled=True)  69.9 us
    reduce_scatter x1, waiting for transfers between devices, local(): lax.psum_scatter(grad_wv, 'fsdp', scatter_dimension=0, tiled=True)  69.5 us
    reduce_scatter x1, waiting for transfers between devices, local(): lax.psum_scatter(grad_wq, 'fsdp', scatter_dimension=0, tiled=True)  69 us
    reduce_scatter x1, waiting for transfers between devices, local(): lax.psum_scatter(grad_wk, 'fsdp', scatter_dimension=0, tiled=True)  69 us
    all_gather x1, waiting for transfers between devices, fetch_weights(): lax.all_gather(down_weight, 'fsdp', axis=1, tiled=True)  57.1 us
    reduce_scatter x1, waiting for transfers between devices, local(): lax.psum_scatter(grad_w_up, 'fsdp', scatter_dimension=0, tiled=True)  52.2 us
  transfers between devices with their start and end apart: 24, of which 20 were waited for; matrix products, arithmetic and copies ran while one was open for 15% of the time, Pallas kernels for 0%

commit v1 on v0

--- a/solution.py
+++ b/solution.py
@@ -341,7 +341,7 @@
     )
     unit_line = jnp.zeros((unit_width * tp_count,), jnp.float32)
     unit_line = lax.dynamic_update_slice_in_dim(unit_line, up_sum, tp_index * unit_width, 0)
-    summed_small = lax.psum((width_stack, head_stack, unit_line), ("fsdp", "tp"))
+    summed_small = lax.psum(lax.psum((width_stack, head_stack, unit_line), "tp"), "fsdp")
     shard_size = model_width // lax.axis_size("fsdp")
     width_pieces = lax.dynamic_slice_in_dim(summed_small[0], fsdp_index * shard_size, shard_size, 1)
     head_pieces = lax.dynamic_slice_in_dim(summed_small[1], tp_index * head_width, head_width, 1)

time: 1300 us -> 1300 us (level)
    psum x1 -> x2, blocking collectives: 43.7 us -> 53.3 us  [the longest x1 42.3 us: local(): lax.psum(lax.psum((width_stack, head_stack, unit_line), 'tp'), 'fsdp')]
where the time goes in v1:
time: 1300 us
  waiting for transfers between devices  820 us (63%)
  blocking collectives  223 us (17%)
  matrix products  156 us (12%)
  other arithmetic  50.1 us (4%)
  local copies, waits for them, and re-layouts  25.8 us (2%)
  between operations  17.3 us (1%)
    unnamed x32, waiting for transfers between devices  205 us
    reduce_scatter x1, waiting for transfers between devices, local(): lax.psum_scatter(grad_w_down, 'fsdp', scatter_dimension=1, tiled=True)  108 us
    reduce_scatter x1, waiting for transfers between devices, local(): lax.psum_scatter(grad_w_out, 'fsdp', scatter_dimension=1, tiled=True)  70 us
    reduce_scatter x1, waiting for transfers between devices, local(): lax.psum_scatter(grad_wv, 'fsdp', scatter_dimension=0, tiled=True)  69.5 us
    reduce_scatter x1, waiting for transfers between devices, local(): lax.psum_scatter(grad_wq, 'fsdp', scatter_dimension=0, tiled=True)  69.4 us
    reduce_scatter x1, waiting for transfers between devices, local(): lax.psum_scatter(grad_wk, 'fsdp', scatter_dimension=0, tiled=True)  69.3 us
    all_gather x1, waiting for transfers between devices, fetch_weights(): lax.all_gather(down_weight, 'fsdp', axis=1, tiled=True)  57.1 us
    dot_general x12, matrix products, plain_dot(): return jnp.dot(left, right, preferred_element_type=jnp.float32)  49.9 us
  transfers between devices with their start and end apart: 24, of which 20 were waited for; matrix products, arithmetic and copies ran while one was open for 15% of the time, Pallas kernels for 0%

profile of v1, /device:TPU:0, one launch (start us, length us, event | category | flops | bytes accessed | tf_op | source)
XLA Modules:
  0.0 1295.7 jit_solution(14003539334269352539)
XLA Ops:
  14.4 38.8 %all-reduce.16 = (bf16[1152]{0:T(1024)(128)(2,1)S(1)}, bf16[1152]{0:T(1024)(128)(2,1)S(1)}, bf16[1152]{0:T(1024)(128)(2,1)S(1)}, bf16[1152]{0:T(1024)(128)(2,1)S...) all-reduce(bf16[1152]{0:T(1024)(128)(2,1)S(1)} %dynamic-update-slic, ...), channel_id=1, replica_groups=mesh['fsdp'=8,'tp'=4] {'fsdp'}, use_global_device_ids=true, to_apply=%add.1 | all-reduce | flops 6912 | bytes 27648
  60.0 32.5 %all_gather.44 = bf16[1152,288]{1,0:T(8,128)(2,1)S(1)} all-gather(bf16[144,288]{1,0:T(8,128)(2,1)S(1)} %copy-done.54), channel_id=1, replica_groups=mesh['fsdp'=8,'tp'=4] {'fsdp'}, dimensions={0}, use_global_device_ids=true | all-gather | bytes 746496 | tf_op jit(solution)/shard_map/all_gather | solution.py:77
  92.5 32.2 %all_gather.45 = bf16[1152,288]{1,0:T(8,128)(2,1)S(1)} all-gather(bf16[144,288]{1,0:T(8,128)(2,1)S(1)} %copy-done.55), channel_id=1, replica_groups=mesh['fsdp'=8,'tp'=4] {'fsdp'}, dimensions={0}, use_global_device_ids=true | all-gather | bytes 746496 | tf_op jit(solution)/shard_map/all_gather | solution.py:78
  126.1 34.5 %all_gather.43 = bf16[1152,288]{1,0:T(8,128)(2,1)} all-gather(bf16[144,288]{1,0:T(8,128)(2,1)S(1)} %copy-done.56), channel_id=1, replica_groups=mesh['fsdp'=8,'tp'=4] {'fsdp'}, dimensions={0}, use_global_device_ids=true | all-gather | bytes 746496 | tf_op jit(solution)/shard_map/all_gather | solution.py:79
  160.6 32.0 %all_gather.46 = bf16[288,1152]{0,1:T(8,128)(2,1)S(1)} all-gather(bf16[288,144]{0,1:T(8,128)(2,1)S(1)} %copy-done.57), channel_id=1, replica_groups=mesh['fsdp'=8,'tp'=4] {'fsdp'}, dimensions={1}, use_global_device_ids=true | all-gather | bytes 746496 | tf_op jit(solution)/shard_map/all_gather | solution.py:80
  231.9 15.1 %reduce-scatter.47.cloned.1.call-done = f32[184,1152]{1,0:T(8,128)} async-done(((f32[736,1152]{1,0:T(8,128)}), f32[184,1152]{1,0:T(8,128)}) %reduce-scatter.47.cloned.1.call-update) | async-done | bytes 847888
  247.0 42.0 %reduce-scatter.43.cloned.1.call-done = f32[184,1152]{1,0:T(8,128)} async-done(((f32[736,1152]{1,0:T(8,128)}), f32[184,1152]{1,0:T(8,128)}) %reduce-scatter.43.cloned.1.call-update) | async-done | bytes 847888
  294.5 16.9 %all-gather.23.cloned.1.call-done = bf16[736,1152]{1,0:T(8,128)(2,1)} async-done(((bf16[184,1152]{1,0:T(8,128)(2,1)}), bf16[736,1152]{1,0:T(8,128)(2,1)}) %all-gather.23.cloned.1.call-update) | async-done | bytes 1695760 | tf_op jit(solution)/shard_map/all_gather | solution.py:194
  311.5 57.1 %all-gather.17.cloned.1.call-done = bf16[1076,1152]{0,1:T(8,128)(2,1)} async-done(((bf16[1076,144]{0,1:T(8,128)(2,1)}), bf16[1076,1152]{0,1:T(8,128)(2,1)}) %all-gather.17.cloned.1.call-update) | async-done | bytes 2479120 | tf_op jit(solution)/shard_map/all_gather | solution.py:87
  368.5 6.4 fusion.87
  375.0 49.4 %all-gather.15.cloned.1.call-done = bf16[1152,1076]{1,0:T(8,128)(2,1)} async-done(((bf16[144,1076]{1,0:T(8,128)(2,1)}), bf16[1152,1076]{1,0:T(8,128)(2,1)}) %all-gather.15.cloned.1.call-update) | async-done | bytes 2479120 | tf_op jit(solution)/shard_map/all_gather | solution.py:86
  424.3 20.5 %all-gather.13.cloned.1.call-done = bf16[736,1152]{1,0:T(8,128)(2,1)} async-done(((bf16[184,1152]{1,0:T(8,128)(2,1)}), bf16[736,1152]{1,0:T(8,128)(2,1)}) %all-gather.13.cloned.1.call-update) | async-done | bytes 1695760 | tf_op jit(solution)/shard_map/all_gather | solution.py:129
  444.9 10.3 convert_reduce_fusion.1
  473.2 15.4 %all-gather.21.cloned.1.call-done = bf16[736,1152]{1,0:T(8,128)(2,1)} async-done(((bf16[184,1152]{1,0:T(8,128)(2,1)}), bf16[736,1152]{1,0:T(8,128)(2,1)}) %all-gather.21.cloned.1.call-update) | async-done | bytes 1695760 | tf_op jit(solution)/shard_map/all_gather | solution.py:129
  488.6 10.2 convert_reduce_fusion
  504.7 7.8 fusion.73
  512.5 7.6 fusion.74
  520.3 10.4 reduce-scatter.51.cloned.1.call-done
  530.6 42.1 %reduce-scatter.55.cloned.1.call-done = f32[184,1152]{1,0:T(8,128)} async-done(((f32[736,1152]{1,0:T(8,128)}), f32[184,1152]{1,0:T(8,128)}) %reduce-scatter.55.cloned.1.call-update) | async-done | bytes 847888
  574.8 39.9 %reduce-scatter.45.cloned.1.call-done = f32[184,1152]{1,0:T(8,128)} async-done(((f32[736,1152]{1,0:T(8,128)}), f32[184,1152]{1,0:T(8,128)}) %reduce-scatter.45.cloned.1.call-update) | async-done | bytes 847888
  614.8 42.1 %reduce-scatter.49.cloned.1.call-done = f32[184,1152]{1,0:T(8,128)} async-done(((f32[736,1152]{1,0:T(8,128)}), f32[184,1152]{1,0:T(8,128)}) %reduce-scatter.49.cloned.1.call-update) | async-done | bytes 847888
  665.4 19.5 %all-gather.29.cloned.1.call-done = bf16[736,1152]{1,0:T(8,128)(2,1)} async-done(((bf16[184,1152]{1,0:T(8,128)(2,1)}), bf16[736,1152]{1,0:T(8,128)(2,1)}) %all-gather.29.cloned.1.call-update) | async-done | bytes 1695760 | tf_op jit(solution)/shard_map/all_gather | solution.py:213
  713.3 6.6 multiply_reduce_fusion.1
  782.2 9.3 reduce-scatter.53.cloned.1.call-done
  796.6 11.0 all-reduce.15
  807.6 42.3 %all-reduce.14 = (f32[6,1152]{1,0:T(8,128)S(1)}, f32[2,1152]{1,0:T(2,128)S(1)}, f32[4304]{0:T(1024)S(1)}) all-reduce(f32[6,1152]{1,0:T(8,128)S(1)} %get-tuple-element.48, f32[2,1152]{1,0:T(2,128)S(1)} %get-tuple-element.49, f32[4304]{0:T(1024)S(1)} %get-tuple-element.50), channel_id=1, replica_groups=mesh['fsdp'=8,'tp'=4] {'fsdp'}, use_global_device_ids=true, to_apply=%region_43.44 | all-reduce | flops 13520 | bytes 108160 | tf_op jit(solution)/shard_map/psum | solution.py:344
  857.5 44.4 %reduce-scatter.39.cloned.1.call-done = f32[144,1076]{1,0:T(8,128)} async-done(((f32[1152,1076]{1,0:T(8,128)}), f32[144,1076]{1,0:T(8,128)}) %reduce-scatter.39.cloned.1.call-update) | async-done | bytes 619792 | tf_op jit(solution)/shard_map/reduce_scatter | solution.py:332
  901.9 108.4 %reduce-scatter.41.cloned.1.call-done = f32[1076,144]{0,1:T(8,128)} async-done(((f32[1076,1152]{0,1:T(8,128)}), f32[1076,144]{0,1:T(8,128)}) %reduce-scatter.41.cloned.1.call-update) | async-done | bytes 619792 | tf_op jit(solution)/shard_map/reduce_scatter | solution.py:333
  1010.4 70.0 %reduce-scatter.37.cloned.1.call-done = f32[288,144]{0,1:T(8,128)} async-done(((f32[288,1152]{0,1:T(8,128)}), f32[288,144]{0,1:T(8,128)}) %reduce-scatter.37.cloned.1.call-update) | async-done | bytes 165904 | tf_op jit(solution)/shard_map/reduce_scatter | solution.py:331
  1080.3 69.5 %reduce-scatter.35.cloned.1.call-done = f32[144,288]{1,0:T(8,128)} async-done(((f32[1152,288]{1,0:T(8,128)}), f32[144,288]{1,0:T(8,128)}) %reduce-scatter.35.cloned.1.call-update) | async-done | bytes 165904 | tf_op jit(solution)/shard_map/reduce_scatter | solution.py:330
  1149.8 69.3 %reduce-scatter.33.cloned.1.call-done = f32[144,288]{1,0:T(8,128)} async-done(((f32[1152,288]{1,0:T(8,128)}), f32[144,288]{1,0:T(8,128)}) %reduce-scatter.33.cloned.1.call-update) | async-done | bytes 165904 | tf_op jit(solution)/shard_map/reduce_scatter | solution.py:329
  1219.1 69.4 %reduce-scatter.31.cloned.1.call-done = f32[144,288]{1,0:T(8,128)} async-done(((f32[1152,288]{1,0:T(8,128)}), f32[144,288]{1,0:T(8,128)}) %reduce-scatter.31.cloned.1.call-update) | async-done | bytes 165904 | tf_op jit(solution)/shard_map/reduce_scatter | solution.py:328
  (416 shorter events, 195.6 us)
Async XLA Ops:
  7.2 85.3 %copy-start.90 = (bf16[288]{0:T(512)(128)(2,1)S(1)}, bf16[288]{0:T(512)(128)(2,1)}, u32[]{:S(2)}) copy-start(bf16[288]{0:T(512)(128)(2,1)} %param.24) | copy-start | bytes 1732
  7.2 117.5 %copy-start.89 = (s32[2]{0:T(128)S(1)}, s32[2]{0:T(128)}, u32[]{:S(2)}) copy-start(s32[2]{0:T(128)} %param.20) | copy-start | bytes 28
  7.2 118.8 %copy-start.56 = (bf16[144,288]{1,0:T(8,128)(2,1)S(1)}, bf16[144,288]{1,0:T(8,128)(2,1)}, u32[]{:S(2)}) copy-start(bf16[144,288]{1,0:T(8,128)(2,1)} %param.26) | copy-start | bytes 248836
  7.2 185.3 %all-gather.19.cloned.1.call-start = ((), (), s32[]{:S(2)}) async-start(), calls=%async_computation.18 | async-start | bytes 2119680 | tf_op jit(solution)/shard_map/all_gather | solution.py:108
  54.6 106.0 %copy-start.91 = (bf16[288]{0:T(512)(128)(2,1)S(1)}, bf16[288]{0:T(512)(128)(2,1)}, u32[]{:S(2)}) copy-start(bf16[288]{0:T(512)(128)(2,1)} %param.27) | copy-start | bytes 1732
  54.6 106.0 %copy-start.57 = (bf16[288,144]{0,1:T(8,128)(2,1)S(1)}, bf16[288,144]{0,1:T(8,128)(2,1)}, u32[]{:S(2)}) copy-start(bf16[288,144]{0,1:T(8,128)(2,1)} %param.28) | copy-start | bytes 248836
  59.2 151.7 %all-gather.11.cloned.1.call-start = ((), (), s32[]{:S(2)}) async-start(), calls=%async_computation.14 | async-start | bytes 2119680 | tf_op jit(solution)/shard_map/all_gather | solution.py:108
  60.0 187.1 %reduce-scatter.47.cloned.1.call-start = ((), (), s32[]{:S(2)}) async-start(), calls=%async_computation.32 | async-start | bytes 4239360
  124.7 86.2 %copy-start.11 = (bf16[1152,288]{1,0:T(8,128)(2,1)}, bf16[1152,288]{1,0:T(8,128)(2,1)S(1)}, u32[]{:S(2)}) copy-start(bf16[1152,288]{1,0:T(8,128)(2,1)S(1)} %all_gather.45) | copy-start | bytes 1990660
  209.9 79.2 %reduce-scatter.43.cloned.1.call-start = ((), (), s32[]{:S(2)}) async-start(), calls=%async_computation.30 | async-start | bytes 4239360
  227.9 83.6 %all-gather.23.cloned.1.call-start = ((), (), s32[]{:S(2)}) async-start(), calls=%async_computation.20 | async-start | bytes 2119680 | tf_op jit(solution)/shard_map/all_gather | solution.py:194
  230.5 138.0 %all-gather.17.cloned.1.call-start = ((), (), s32[]{:S(2)}) async-start(), calls=%async_computation.17 | async-start | bytes 2985984 | tf_op jit(solution)/shard_map/all_gather | solution.py:87
  231.1 193.3 %all-gather.15.cloned.1.call-start = ((), (), s32[]{:S(2)}) async-start(), calls=%async_computation.16 | async-start | bytes 2985984 | tf_op jit(solution)/shard_map/all_gather | solution.py:86
  231.8 213.0 %all-gather.13.cloned.1.call-start = ((), (), s32[]{:S(2)}) async-start(), calls=%async_computation.15 | async-start | bytes 2119680 | tf_op jit(solution)/shard_map/all_gather | solution.py:129
  292.7 174.2 %all-gather.27.cloned.1.call-start = ((), (), s32[]{:S(2)}) async-start(), calls=%async_computation.22 | async-start | bytes 2119680 | tf_op jit(solution)/shard_map/all_gather | solution.py:194
  293.4 195.2 %all-gather.21.cloned.1.call-start = ((), (), s32[]{:S(2)}) async-start(), calls=%async_computation.19 | async-start | bytes 2119680 | tf_op jit(solution)/shard_map/all_gather | solution.py:129
  294.0 236.7 %reduce-scatter.51.cloned.1.call-start = ((), (), s32[]{:S(2)}) async-start(), calls=%async_computation.34 | async-start | bytes 4239360
  460.9 111.8 %reduce-scatter.55.cloned.1.call-start = ((), (), s32[]{:S(2)}) async-start(), calls=%async_computation.36 | async-start | bytes 4239360
  504.4 110.4 %reduce-scatter.45.cloned.1.call-start = ((), (), s32[]{:S(2)}) async-start(), calls=%async_computation.31 | async-start | bytes 4239360
  512.5 144.4 %reduce-scatter.49.cloned.1.call-start = ((), (), s32[]{:S(2)}) async-start(), calls=%async_computation.33 | async-start | bytes 4239360
  520.2 164.7 %all-gather.29.cloned.1.call-start = ((), (), s32[]{:S(2)}) async-start(), calls=%async_computation.23 | async-start | bytes 2119680 | tf_op jit(solution)/shard_map/all_gather | solution.py:213
  574.8 86.5 %copy-start.72 = (f32[184]{0:T(256)S(1)}, f32[184]{0:T(256)}, u32[]{:S(2)}) copy-start(f32[184]{0:T(256)} %copy-done.71) | copy-start | bytes 2212
  574.8 86.5 %copy-start.74 = (f32[184]{0:T(256)S(1)}, f32[184]{0:T(256)}, u32[]{:S(2)}) copy-start(f32[184]{0:T(256)} %copy-done.73) | copy-start | bytes 2212
  664.4 45.7 %all-gather.25.cloned.1.call-start = ((), (), s32[]{:S(2)}) async-start(), calls=%async_computation.21 | async-start | bytes 2119680 | tf_op jit(solution)/shard_map/all_gather | solution.py:213
  665.0 117.2 %reduce-scatter.57.cloned.1.call-start = ((), (), s32[]{:S(2)}) async-start(), calls=%async_computation.37 | async-start | bytes 4239360
  709.8 81.7 %reduce-scatter.53.cloned.1.call-start = ((), (), s32[]{:S(2)}) async-start(), calls=%async_computation.35 | async-start | bytes 4239360
  734.7 167.2 %reduce-scatter.39.cloned.1.call-start = ((), (), s32[]{:S(2)}) async-start(), calls=%async_computation.28 | async-start | bytes 5971968 | tf_op jit(solution)/shard_map/reduce_scatter | solution.py:332
  745.5 264.8 %reduce-scatter.41.cloned.1.call-start = ((), (), s32[]{:S(2)}) async-start(), calls=%async_computation.29 | async-start | bytes 5971968 | tf_op jit(solution)/shard_map/reduce_scatter | solution.py:333
  756.9 323.5 %reduce-scatter.37.cloned.1.call-start = ((), (), s32[]{:S(2)}) async-start(), calls=%async_computation.27 | async-start | bytes 1990656 | tf_op jit(solution)/shard_map/reduce_scatter | solution.py:331
  763.1 386.7 %reduce-scatter.35.cloned.1.call-start = ((), (), s32[]{:S(2)}) async-start(), calls=%async_computation.26 | async-start | bytes 1990656 | tf_op jit(solution)/shard_map/reduce_scatter | solution.py:330
  768.3 450.8 %reduce-scatter.33.cloned.1.call-start = ((), (), s32[]{:S(2)}) async-start(), calls=%async_computation.25 | async-start | bytes 1990656 | tf_op jit(solution)/shard_map/reduce_scatter | solution.py:329
  773.6 514.9 %reduce-scatter.31.cloned.1.call-start = ((), (), s32[]{:S(2)}) async-start(), calls=%async_computation.24 | async-start | bytes 1990656 | tf_op jit(solution)/shard_map/reduce_scatter | solution.py:328
  (105 other events, 985.4 us)
Sparse Core Ops, SparseCore 0:
  59.3 17.5 all-gather.18
  79.1 20.3 all-gather.10
  210.0 36.9 reduce-scatter.46
  249.6 39.4 reduce-scatter.42
  291.1 20.3 all-gather.22
  313.5 55.0 all-gather.16
  370.7 53.5 all-gather.14
  425.9 18.9 all-gather.12
  446.4 20.3 all-gather.26
  468.2 20.3 all-gather.20
  491.1 39.4 reduce-scatter.50
  533.2 39.4 reduce-scatter.54
  575.2 39.4 reduce-scatter.44
  617.3 39.4 reduce-scatter.48
  664.5 20.3 all-gather.28
  686.3 20.3 all-gather.24
  709.9 39.4 reduce-scatter.56
  752.0 39.4 reduce-scatter.52
  795.7 106.1 reduce-scatter.38
  906.4 103.9 reduce-scatter.40
  1014.4 65.8 reduce-scatter.36
  1084.8 64.9 reduce-scatter.34
  1153.8 65.2 reduce-scatter.32
  1223.4 65.0 reduce-scatter.30
